TPU v7x, 32 devices: a whole 2x2x4 slice. The times are simulated.
32 devices in a mesh: parts: 2 (over y), tensor: 4 (over z), dp: 4 (over x, core).
Axes of the slice: x: 2, y: 2, z: 4, core: 2. Of those that a mesh axis runs over, the one named last changes fastest.
Arguments:
- inputs: bfloat16 [4096, 8192], P(('parts', 'dp'), 'tensor'), parts along dimension 0, may hold values from -6 to 6
- cotangent: bfloat16 [4096, 8192], P(('parts', 'dp'), 'tensor'), parts along dimension 0, may hold values from -6 to 6
- weight: bfloat16 [8192, 8192], P(None, 'tensor'), may hold values from -0.0625 to 0.0625
- down_weight_maps: bfloat16 [8192, 2048], P('tensor', 'parts'), parts along dimension 1, may hold values from -0.0625 to 0.0625
- up_weight_maps: bfloat16 [2048, 8192], P('parts', 'tensor'), parts along dimension 0, may hold values from -0.75 to 0.75
- counts: int32 [8, 16], P('parts'), parts along dimension 0, may hold values from 0 to 256, as said below
- ranks: int32 [32], P('parts'), parts along dimension 0, may hold values from 8 to 64, as said below
- owners: int32 [32], P('parts'), parts along dimension 0, may hold values from 0 to 3
Outputs:
- projected: bfloat16 [4096, 8192], P(('parts', 'dp'), 'tensor'), parts along dimension 0
- input_grad: bfloat16 [4096, 8192], P(('parts', 'dp'), 'tensor'), parts along dimension 0
- grad_a: float32 [8, 8192, 1024], P(('parts', 'dp'), 'tensor'), parts along dimension 0
- grad_b: float32 [8, 1024, 8192], P(('parts', 'dp'), None, 'tensor'), parts along dimension 0
There are 2 independent parts, one for each index of `parts`. A program takes and returns all parts, laid end to end along the dimension named above; an argument that names none is the same for every part. Nothing has to cross between parts.
Inputs may be any that keep to these rules, and one draw needn't show every extreme that they name: `counts`: each row sums to at most 512, one row to exactly 512, and all rows together to exactly 1024; some entry is exactly 256. `ranks`: each rank is 64 divided by 1, 2, 4 or 8; some trial has 64 and some 64 // 8.
All inputs are finite; a program needn't handle non-finite values.
Results may differ from a plain program's by a relative error of at most 0.0034.
Values may be sent and summed in bfloat16 or wider, within the bound.
A program may use at most 256 MiB of HBM per device.

v0:
```python
import jax
import jax.numpy as jnp
from jax import lax
from jax.sharding import PartitionSpec as P

LARGEST_RANK = 64
TRIALS = 16
adapter_alpha = 16.0


def local(inputs, cotangent, weight, down_weight_maps, up_weight_maps, counts, ranks, owners):
    slot_count, feature_local = inputs.shape
    group_count = counts.shape[0]
    adapter_rank_width = down_weight_maps.shape[1]
    column = jnp.arange(adapter_rank_width, dtype=jnp.int32)
    col_trial = column // LARGEST_RANK
    column_slot = column % LARGEST_RANK
    trial_ids = jnp.arange(TRIALS, dtype=jnp.int32)
    matches = col_trial[:, None] == trial_ids[None, :]
    rank_per_column = jnp.sum(jnp.where(matches, ranks[None, :], 0), axis=1)
    owner_col = jnp.sum(jnp.where(matches, owners[None, :], 0), axis=1)
    scale_per_column = jnp.where(
        column_slot < rank_per_column, adapter_alpha / rank_per_column.astype(jnp.float32), 0.0
    )
    trial_rows = jnp.sum(counts, axis=0)
    per_trial = 1.0 / jnp.maximum(trial_rows, 1).astype(jnp.float32)
    inverse_col = jnp.sum(jnp.where(matches, per_trial[None, :], 0.0), axis=1)
    cumulative = jnp.cumsum(counts, axis=1)
    group_ids = jnp.arange(group_count, dtype=jnp.int32)
    my_group = lax.axis_index("dp")
    contract_trailing = (((1,), (1,)), ((), ()))
    contract_first = (((0,), (0,)), ((), ()))
    positions = jnp.arange(slot_count, dtype=jnp.int32)
    my_bounds = jnp.sum(jnp.where((group_ids == my_group)[:, None], cumulative, 0), axis=0)
    row_trial = jnp.sum((positions[:, None] >= my_bounds[None, :]).astype(jnp.int32), axis=1)
    is_live = row_trial < TRIALS
    coef = jnp.where(row_trial[:, None] == col_trial[None, :], scale_per_column[None, :], 0.0)
    frozen_output = jnp.dot(
        lax.all_gather(inputs, "tensor", axis=1, tiled=True),
        weight,
        preferred_element_type=jnp.float32,
    )
    down_projected_sum = lax.psum(
        jnp.dot(inputs, down_weight_maps, preferred_element_type=jnp.float32), "tensor"
    )
    scaled_down_projected = (coef * down_projected_sum).astype(jnp.bfloat16)
    merged_output = frozen_output + jnp.dot(
        scaled_down_projected, up_weight_maps, preferred_element_type=jnp.float32
    )
    result = jnp.where(is_live[:, None], merged_output, 0.0).astype(jnp.bfloat16)
    back_part = lax.dot_general(
        cotangent, up_weight_maps, contract_trailing, preferred_element_type=jnp.float32
    )
    back_sum = lax.psum(back_part, "tensor")
    scaled_up_projected = (coef * back_sum).astype(jnp.bfloat16)
    frozen_back = lax.dot_general(
        cotangent, weight, contract_trailing, preferred_element_type=jnp.float32
    )
    frozen_share = lax.psum_scatter(frozen_back, "tensor", scatter_dimension=1, tiled=True)
    adapter_in = lax.dot_general(
        scaled_up_projected, down_weight_maps, contract_trailing, preferred_element_type=jnp.float32
    )
    gradient = jnp.where(is_live[:, None], frozen_share + adapter_in, 0.0).astype(jnp.bfloat16)
    term_a = (
        lax.dot_general(
            inputs, scaled_up_projected, contract_first, preferred_element_type=jnp.float32
        )
        * inverse_col[None, :]
    )
    term_b = (
        lax.dot_general(
            scaled_down_projected, cotangent, contract_first, preferred_element_type=jnp.float32
        )
        * inverse_col[:, None]
    )
    projected, input_grad, term_a, term_b = (result, gradient, term_a, term_b)
    full_a, full_b = lax.psum((term_a, term_b), "dp")
    owned_mine = (owner_col == my_group).astype(jnp.float32)
    grad_a = (full_a * owned_mine[None, :])[None]
    grad_b = (full_b * owned_mine[:, None])[None]
    return (projected, input_grad, grad_a, grad_b)


def solution(mesh):
    return jax.shard_map(
        local,
        mesh=mesh,
        in_specs=(
            P(("parts", "dp"), "tensor"),
            P(("parts", "dp"), "tensor"),
            P(None, "tensor"),
            P("tensor", "parts"),
            P("parts", "tensor"),
            P("parts", None),
            P("parts"),
            P("parts"),
        ),
        out_specs=(
            P(("parts", "dp"), "tensor"),
            P(("parts", "dp"), "tensor"),
            P(("parts", "dp"), "tensor", None),
            P(("parts", "dp"), None, "tensor"),
        ),
        check_vma=False,
    )
```

profile of v0, /device:TPU:0, one launch (start us, length us, event | category | flops | bytes accessed | tf_op | source)
XLA Modules:
  0.0 924.6 jit_solution(6488323135650758244)
XLA Ops:
  7.2 0.0 copy-start
  7.2 0.0 all-reduce.7.cloned.1.call-start
  7.2 0.0 copy-start.7
  7.2 6.6 fusion.15
  13.9 3.7 fusion.17
  17.6 0.0 all-reduce.7.cloned.1.call-update
  17.6 0.0 all-reduce.5.cloned.1.call-start
  17.6 0.6 copy-done.4
  18.2 0.2 reduce_window_sum.11
  18.5 0.1 select_reduce_fusion.3
  18.5 0.1 convert_reduce_fusion
  18.6 0.1 select_reduce_fusion.1
  18.8 0.1 select_reduce_fusion
  18.9 156.9 %all-reduce.7.cloned.1.call-done = (f32[512,1024]{1,0:T(8,128)}, f32[512,1024]{1,0:T(8,128)}) async-done(((f32[512,1024]{1,0:T(8,128)}, f32[512,1024]{1,0:T(8,128)}), (f32[512,1024]{1,0:T(8,128)}, f32[512,1024]{1,0:T(8,128)})) %all-reduce.7.cloned.1.call-update) | async-done | bytes 4194320 | tf_op jit(solution)/shard_map/psum | solution.py:43
  175.8 8.2 multiply_bitcast_fusion.2
  184.0 5.9 convolution_multiply_fusion
  189.9 0.0 all-reduce.5.cloned.1.call-update
  190.0 0.0 all-gather.2.cloned.1.call-start
  190.0 0.7 all-gather.2.cloned.1.call-update
  190.7 0.2 reduce-scatter.2.cloned.1.call-start
  190.9 25.8 %fusion.16 = f32[512,8192]{1,0:T(8,128)} fusion(bf16[512,2048]{1,0:T(8,128)(2,1)S(1)} %copy-done, bf16[8192,2048]{1,0:T(8,128)(2,1)} %param.10), kind=kOutput, calls=%fused_computation.36 | convolution fusion | flops 17179869184 | bytes 52428800 | tf_op jit(solution)/shard_map/dot_general | solution.py:56
  216.7 0.0 reduce-scatter.2.cloned.1.call-update
  216.8 1.6 copy-done.3
  218.4 6.5 fusion.13
  224.9 253.1 %all-reduce.5.cloned.1.call-done = (f32[2048,1024]{0,1:T(8,128)}, f32[1024,2048]{1,0:T(8,128)}) async-done(((f32[2048,1024]{0,1:T(8,128)}, f32[1024,2048]{1,0:T(8,128)}), (f32[2048,1024]{0,1:T(8,128)}, f32[1024,2048]{1,0:T(8,128)})) %all-reduce.5.cloned.1.call-update) | async-done | bytes 16777232 | tf_op jit(solution)/shard_map/psum | solution.py:77
  478.0 7.4 multiply_bitcast_fusion.1
  485.3 9.7 %copy.13 = f32[1,2048,1024]{2,1,0:T(8,128)} copy(f32[1,2048,1024]{1,2,0:T(8,128)} %multiply_bitcast_fusion.1) | data formatting | bytes 16777216
  495.1 7.4 multiply_bitcast_fusion
  502.5 126.8 %all-gather.2.cloned.1.call-done = bf16[512,8192]{1,0:T(8,128)(2,1)} async-done(((bf16[512,2048]{1,0:T(8,128)(2,1)}), bf16[512,8192]{1,0:T(8,128)(2,1)}) %all-gather.2.cloned.1.call-update) | async-done | bytes 8388624 | tf_op jit(solution)/shard_map/all_gather | solution.py:39
  629.3 24.9 %select_convert_fusion.1 = bf16[512,2048]{1,0:T(8,128)(2,1)} fusion(f32[512,2048]{1,0:T(8,128)} %fusion.13, bf16[512,8192]{1,0:T(8,128)(2,1)} %all-gather.2.cloned.1.call-done, bf16[8192,2048]{1,0:T(8,128)(2,1)} %param.10, pred[512]{0:T(512)(128)(4,1)S(1)} %broadcast_compare_fusion), kind=kOutput, calls=%fused_computation.5 | convolution fusion | flops 17183014912 | bytes 48235008 | tf_op jit(solution)/shard_map/dot_general | solution.py:38
  654.2 255.9 %reduce-scatter.2.cloned.1.call-done = f32[512,2048]{1,0:T(8,128)} async-done(((f32[512,8192]{1,0:T(8,128)}), f32[512,2048]{1,0:T(8,128)}) %reduce-scatter.2.cloned.1.call-update) | async-done | bytes 4194320 | tf_op jit(solution)/shard_map/reduce_scatter | solution.py:59
  910.1 7.9 select_convert_fusion
  (19 shorter events, 0.1 us)
Async XLA Ops:
  7.2 6.7 copy-start
  7.2 168.6 %all-reduce.7.cloned.1.call-start = ((), (), s32[]{:S(2)}) async-start(), calls=%async_computation.4 | async-start | bytes 8388608 | tf_op jit(solution)/shard_map/psum | solution.py:43
  7.2 6.6 copy-start.7
  17.5 0.7 copy-start.4
  17.6 1.2 copy-start.5
  17.6 1.2 copy-start.6
  17.6 460.4 %all-reduce.5.cloned.1.call-start = ((), (), s32[]{:S(2)}) async-start(), calls=%async_computation.3 | async-start | bytes 33554432 | tf_op jit(solution)/shard_map/psum | solution.py:77
  175.8 8.3 copy-start.2
  190.0 439.3 %all-gather.2.cloned.1.call-start = ((), (), s32[]{:S(2)}) async-start(), calls=%async_computation.1 | async-start | bytes 10485760 | tf_op jit(solution)/shard_map/all_gather | solution.py:39
  190.7 719.4 %reduce-scatter.2.cloned.1.call-start = ((), (), s32[]{:S(2)}) async-start(), calls=%async_computation.2 | async-start | bytes 20971520 | tf_op jit(solution)/shard_map/reduce_scatter | solution.py:59
  216.7 1.7 copy-start.3
  910.1 7.9 copy-start.1
Sparse Core Ops, SparseCore 0:
  17.7 158.0 all-reduce.6
  190.1 287.8 all-reduce.4
  479.6 149.6 all-gather.1
  631.6 278.4 reduce-scatter.1
where the time goes:
time: 925 us
  waiting for transfers between devices  793 us (86%)
  matrix products  89.6 us (10%)
  other arithmetic  15.4 us (2%)
  between operations  13.9 us (2%)
  local copies, waits for them, and re-layouts  12 us (1%)
    reduce_scatter x1, waiting for transfers between devices, local(): lax.psum_scatter(frozen_back, 'tensor', scatter_dimension=1, tiled=True)  256 us
    psum x1, waiting for transfers between devices, local(): full_a, full_b = lax.psum((term_a, term_b), 'dp')  253 us
    psum x1, waiting for transfers between devices, local(): lax.psum(jnp.dot(inputs, down_weight_maps, preferred_element_type=jnp.flo...  157 us
    all_gather x1, waiting for transfers between devices, local(): lax.all_gather(inputs, 'tensor', axis=1, tiled=True)  127 us
    dot_general x1, matrix products, local(): lax.dot_general(cotangent, weight, contract_trailing, preferred_element_t...  25.8 us
    dot_general x1, matrix products, local(): jnp.dot(lax.all_gather(inputs, 'tensor', axis=1, tiled=True), weight, pre...  24.9 us
  transfers between devices with their start and end apart: 4, of which 4 were waited for; matrix products, arithmetic and copies ran while one was open for 9% of the time, Pallas kernels for 0%

commit v1 on v0

--- a/solution.py
+++ b/solution.py
@@ -6,6 +6,28 @@
 LARGEST_RANK = 64
 TRIALS = 16
 adapter_alpha = 16.0
+
+
+def laid_out(parts, dim):
+    parts = jnp.moveaxis(parts, 0, dim)
+    lengths = parts.shape
+    return parts.reshape(*lengths[:dim], lengths[dim] * lengths[dim + 1], *lengths[dim + 2 :])
+
+
+def doubled(x, axis):
+    peers = lax.axis_size(axis)
+    tiles = x[None]
+    for level in range(peers.bit_length() - 1):
+        bit = 1 << level
+        other = lax.ppermute(tiles, axis, [(i, i ^ bit) for i in range(peers)])
+        both = jnp.stack([tiles, other])
+        upper = lax.axis_index(axis) >> level & 1
+        tiles = jnp.where(upper == 0, both, both[::-1]).reshape(-1, *x.shape)
+    return tiles
+
+
+def collect(shard, axis, dim):
+    return laid_out(doubled(shard, axis), dim)
 
 
 def local(inputs, cotangent, weight, down_weight_maps, up_weight_maps, counts, ranks, owners):
@@ -36,9 +58,7 @@
     is_live = row_trial < TRIALS
     coef = jnp.where(row_trial[:, None] == col_trial[None, :], scale_per_column[None, :], 0.0)
     frozen_output = jnp.dot(
-        lax.all_gather(inputs, "tensor", axis=1, tiled=True),
-        weight,
-        preferred_element_type=jnp.float32,
+        collect(inputs, "tensor", 1), weight, preferred_element_type=jnp.float32
     )
     down_projected_sum = lax.psum(
         jnp.dot(inputs, down_weight_maps, preferred_element_type=jnp.float32), "tensor"

time: 925 us -> 776 us (0.84)
  waiting for transfers between devices: 793 us -> 604 us
  other arithmetic: 15.4 us -> 43 us
  local copies, waits for them, and re-layouts: 12 us -> 22.8 us
    psum x1, waiting for transfers between devices: 253 us -> 0.01 us  [local(): full_a, full_b = lax.psum((term_a, term_b), 'dp')]
    ppermute x0 -> x2, waiting for transfers between devices: none -> 222 us  [doubled(): other = lax.ppermute(tiles, axis, [(i, i ^ bit) for i in range(peers)])]
    all_gather x1 -> x0, waiting for transfers between devices: 127 us -> none  [local(): lax.all_gather(inputs, 'tensor', axis=1, tiled=True)]
    reduce_scatter x1, waiting for transfers between devices: 256 us -> 225 us  [local(): lax.psum_scatter(frozen_back, 'tensor', scatter_dimension=1, tiled=True)]
    select_n x0 -> x1, other arithmetic: none -> 14.4 us  [doubled(): tiles = jnp.where(upper == 0, both, both[::-1]).reshape(-1, *x.shape)]
    another operation x0 -> x3, other arithmetic: none -> 13.3 us  [doubled(): both = jnp.stack([tiles, other])]
    select_n x0 -> x1, local copies, waits for them, and re-layouts: none -> 11.4 us  [doubled(): tiles = jnp.where(upper == 0, both, both[::-1]).reshape(-1, *x.shape)]
  transfers between devices with their start and end apart: 4 -> 5, of which waited for: 4 -> 4; matrix products, arithmetic and copies ran while one was open for 9% -> 16% of each run, Pallas kernels for 0% -> 0%
where the time goes in v1:
time: 776 us; the launch traced here: 775 us
  waiting for transfers between devices  604 us (78%)
  matrix products  89.4 us (12%)
  other arithmetic  43 us (6%)
  local copies, waits for them, and re-layouts  22.8 us (3%)
  between operations  13.9 us (2%)
    reduce_scatter x1, waiting for transfers between devices, local(): lax.psum_scatter(frozen_back, 'tensor', scatter_dimension=1, tiled=True)  225 us
    ppermute x2, waiting for transfers between devices, doubled(): other = lax.ppermute(tiles, axis, [(i, i ^ bit) for i in range(peers)])  222 us
    psum x1, waiting for transfers between devices, local(): lax.psum(jnp.dot(inputs, down_weight_maps, preferred_element_type=jnp.flo...  157 us
    dot_general x1, matrix products, local(): jnp.dot(collect(inputs, 'tensor', 1), weight, preferred_element_type=jnp....  25.6 us
    dot_general x1, matrix products, local(): lax.dot_general(cotangent, weight, contract_trailing, preferred_element_t...  25.1 us
  transfers between devices with their start and end apart: 5, of which 4 were waited for; matrix products, arithmetic and copies ran while one was open for 16% of the time, Pallas kernels for 0%

profile of v1, /device:TPU:0, one launch (start us, length us, event | category | flops | bytes accessed | tf_op | source)
XLA Modules:
  0.0 774.9 jit_solution(3674183715210247501)
XLA Ops:
  7.2 0.0 all-reduce.7.cloned.1.call-start
  7.2 6.6 fusion.17
  13.9 3.7 fusion.19
  17.6 0.0 all-reduce.7.cloned.1.call-update
  17.6 0.0 all-reduce.5.cloned.1.call-start
  17.6 0.6 copy-done.6
  18.2 0.2 reduce_window_sum.11
  18.5 0.1 select_reduce_fusion.3
  18.5 0.1 convert_reduce_fusion
  18.6 0.1 select_reduce_fusion.1
  18.8 0.1 select_reduce_fusion
  18.9 156.9 %all-reduce.7.cloned.1.call-done = (f32[512,1024]{1,0:T(8,128)}, f32[512,1024]{1,0:T(8,128)}) async-done(((f32[512,1024]{1,0:T(8,128)}, f32[512,1024]{1,0:T(8,128)}), (f32[512,1024]{1,0:T(8,128)}, f32[512,1024]{1,0:T(8,128)})) %all-reduce.7.cloned.1.call-update) | async-done | bytes 4194320 | tf_op jit(solution)/shard_map/psum | solution.py:63
  175.8 8.1 %multiply_bitcast_fusion.2 = f32[2048,1024]{0,1:T(8,128)} fusion(bf16[512,2048]{1,0:T(8,128)(2,1)} %param.8, f32[1024]{0:T(1024)S(1)} %select_reduce_fusion.1, f32[512,1024]{1,0:T(8,128)} %get-tuple-element.21, f32[1024]{0:T(1024)S(1)} %divide_select_fusion, s32[1024]{0:T(1024)S(1)} %add_select_fusion, s32[512]{0:T(512)S(1)} %convert_reduce_fusion), kind=kOutput, calls=%fused_computation.4 | convolution fusion | flops 2151677952 | bytes 12597248 | tf_op jit(solution)/shard_map/dot_general | solution.py:85
  183.8 5.7 convolution_multiply_fusion
  189.6 0.2 reduce-scatter.2.cloned.1.call-start
  189.8 25.1 %fusion.18 = f32[512,8192]{1,0:T(8,128)} fusion(bf16[512,2048]{1,0:T(8,128)(2,1)S(1)} %copy-done, bf16[8192,2048]{1,0:T(8,128)(2,1)} %param.10), kind=kOutput, calls=%fused_computation.42 | convolution fusion | flops 17179869184 | bytes 52428800 | tf_op jit(solution)/shard_map/dot_general | solution.py:76
  215.0 1.6 copy-done.3
  216.5 47.4 %collective-permute-done = bf16[1,512,2048]{2,1,0:T(8,128)(2,1)} collective-permute-done((bf16[1,512,2048]{2,1,0:T(8,128)(2,1)S(1)}, bf16[1,512,2048]{2,1,0:T(8,128)(2,1)}, u32[]{:S(2)}, u32[]{:S(2)}) %collective-permute-start) | collective-permute-done | bytes 2097184 | tf_op jit(solution)/shard_map/ppermute | solution.py:22
  264.0 2.0 pad_maximum_fusion.1
  265.9 5.0 fusion.1
  270.9 1.4 collective-permute-start.1
  272.4 6.7 fusion.15
  279.0 174.3 %collective-permute-done.1 = bf16[2,512,2048]{2,1,0:T(8,128)(2,1)} collective-permute-done((bf16[2,512,2048]{2,1,0:T(8,128)(2,1)}, bf16[2,512,2048]{2,1,0:T(8,128)(2,1)}, u32[]{:S(2)}, u32[]{:S(2)}) %collective-permute-start.1) | collective-permute-done | bytes 4194336 | tf_op jit(solution)/shard_map/ppermute | solution.py:22
  453.4 6.4 pad_maximum_fusion
  459.7 14.4 %reverse_select_fusion = bf16[2,2,512,2048]{3,2,1,0:T(8,128)(2,1)} fusion(bf16[2,2,512,2048]{3,2,1,0:T(8,128)(2,1)} %pad_maximum_fusion, pred[]{:T(512)S(6)} %eq.72), kind=kLoop, calls=%fused_computation | loop fusion | flops 4194304 | bytes 16777216 | tf_op jit(solution)/shard_map/jit(_where)/select_n | solution.py:25
  474.1 11.4 %copy.15 = bf16[2,2,512,2048]{2,3,1,0:T(8,128)(2,1)} copy(bf16[2,2,512,2048]{3,2,1,0:T(8,128)(2,1)} %reverse_select_fusion) | data formatting | bytes 16777216 | tf_op jit(solution)/shard_map/jit(_where)/select_n | solution.py:25
  485.5 25.6 %select_convert_fusion.1 = bf16[512,2048]{1,0:T(8,128)(2,1)} fusion(f32[512,2048]{1,0:T(8,128)} %fusion.15, bf16[512,8192]{0,1:T(8,128)(2,1)} %bitcast.31, bf16[8192,2048]{1,0:T(8,128)(2,1)} %param.10, pred[512]{0:T(512)(128)(4,1)S(1)} %broadcast_compare_fusion), kind=kOutput, calls=%fused_computation.9 | convolution fusion | flops 17183014912 | bytes 48235008 | tf_op jit(solution)/shard_map/dot_general | solution.py:60
  511.1 7.4 multiply_bitcast_fusion.1
  518.4 9.2 %copy.16 = f32[1,2048,1024]{2,1,0:T(8,128)} copy(f32[1,2048,1024]{1,2,0:T(8,128)} %multiply_bitcast_fusion.1) | data formatting | bytes 16777216
  527.7 7.4 multiply_bitcast_fusion
  535.1 225.3 %reduce-scatter.2.cloned.1.call-done = f32[512,2048]{1,0:T(8,128)} async-done(((f32[512,8192]{1,0:T(8,128)}), f32[512,2048]{1,0:T(8,128)}) %reduce-scatter.2.cloned.1.call-update) | async-done | bytes 4194320 | tf_op jit(solution)/shard_map/reduce_scatter | solution.py:79
  760.4 7.9 %select_convert_fusion = bf16[512,2048]{1,0:T(8,128)(2,1)} fusion(f32[512,2048]{1,0:T(8,128)} %reduce-scatter.2.cloned.1.call-done, bf16[2048,1024]{1,0:T(8,128)(2,1)} %param.11, pred[512]{0:T(512)(128)(4,1)S(1)} %broadcast_compare_fusion, f32[512,1024]{1,0:T(8,128)} %get-tuple-element.21, f32[1024]{0:T(1024)S(1)} %divide_select_fusion, ...), kind=kOutput, calls=%fused_computation.8 | convolution fusion | flops 2152726528 | bytes 12593664 | tf_op jit(solution)/shard_map/dot_general | solution.py:80
  (29 shorter events, 0.1 us)
Async XLA Ops:
  7.2 6.7 copy-start
  7.2 168.6 %all-reduce.7.cloned.1.call-start = ((), (), s32[]{:S(2)}) async-start(), calls=%async_computation.3 | async-start | bytes 8388608 | tf_op jit(solution)/shard_map/psum | solution.py:63
  7.2 6.6 copy-start.9
  17.5 0.7 copy-start.6
  17.6 1.2 copy-start.7
  17.6 1.2 copy-start.8
  17.6 493.5 %all-reduce.5.cloned.1.call-start = ((), (), s32[]{:S(2)}) async-start(), calls=%async_computation.2 | async-start | bytes 33554432 | tf_op jit(solution)/shard_map/psum | solution.py:97
  175.8 8.1 %copy-start.4 = (f32[512,1024]{1,0:T(8,128)S(1)}, f32[512,1024]{1,0:T(8,128)}, u32[]{:S(2)}) copy-start(f32[512,1024]{1,0:T(8,128)} %get-tuple-element.20) | copy-start | bytes 6291460
  189.6 570.8 %reduce-scatter.2.cloned.1.call-start = ((), (), s32[]{:S(2)}) async-start(), calls=%async_computation.1 | async-start | bytes 20971520 | tf_op jit(solution)/shard_map/reduce_scatter | solution.py:79
  214.9 1.6 copy-start.3
  216.5 47.4 %collective-permute-start = (bf16[1,512,2048]{2,1,0:T(8,128)(2,1)S(1)}, bf16[1,512,2048]{2,1,0:T(8,128)(2,1)}, u32[]{:S(2)}, u32[]{:S(2)}) collective-permute-start(bf16[1,512,2048]{2,1,0:T(8,128)(2,1)S(1)} %bitcast.32), channel_id=1, source_target_pairs={{0,4},{4,0},{8,12},{12,8},{1,5},{5,1},{9,13},{13,9},{2,6},{6,2},{1... | collective-permute-start | bytes 6291464 | tf_op jit(solution)/shard_map/ppermute | solution.py:22
  265.9 6.4 copy-start.5
  270.9 182.5 %collective-permute-start.1 = (bf16[2,512,2048]{2,1,0:T(8,128)(2,1)}, bf16[2,512,2048]{2,1,0:T(8,128)(2,1)}, u32[]{:S(2)}, u32[]{:S(2)}) collective-permute-start(bf16[2,512,2048]{2,1,0:T(8,128)(2,1)} %get-tuple-element.23), channel_id=1, source_target_pairs={{0,8},{4,12},{8,0},{12,4},{1,9},{5,13},{9,1},{13,5},{2,10},{6,14},... | collective-permute-start | bytes 12582920 | tf_op jit(solution)/shard_map/ppermute | solution.py:22
  272.4 181.0 %copy-start.2 = (bf16[1,2,512,2048]{3,2,1,0:T(8,128)(2,1)S(1)}, bf16[1,2,512,2048]{3,2,1,0:T(8,128)(2,1)}, u32[]{:S(2)}) copy-start(bf16[1,2,512,2048]{3,2,1,0:T(8,128)(2,1)} %get-tuple-element.22) | copy-start | bytes 12582916
  760.4 7.9 %copy-start.1 = (bf16[512,2048]{1,0:T(8,128)(2,1)S(1)}, bf16[512,2048]{1,0:T(8,128)(2,1)}, u32[]{:S(2)}) copy-start(bf16[512,2048]{1,0:T(8,128)(2,1)} %param.9) | copy-start | bytes 6291460
Sparse Core Ops, SparseCore 0:
  17.7 158.0 all-reduce.6
  189.7 287.8 all-reduce.4
  480.0 280.3 reduce-scatter.1
